TPU v7x, 32 devices: a whole 2x2x4 slice. The times are simulated.
32 devices in a mesh: dp: 8 (over z, y), tensor: 4 (over x, core).
Axes of the slice: x: 2, y: 2, z: 4, core: 2. Of those that a mesh axis runs over, the one named last changes fastest.
Arguments:
- tokens: bfloat16 [8, 512, 768], P('dp'), may hold values from -6 to 6
- cotangent: bfloat16 [8, 512, 768], P('dp'), may hold values from -6 to 6
- norm_gain: float32 [768], replicated, may hold values from 0.1 to 1.9
- w_z: bfloat16 [768, 1536], P(None, 'tensor'), may hold values from -0.21875 to 0.21875
- w_x: bfloat16 [768, 1536], P(None, 'tensor'), may hold values from -0.21875 to 0.21875
- w_bc: bfloat16 [768, 256], replicated, may hold values from -0.21875 to 0.21875
- w_dt: bfloat16 [768, 24], P(None, 'tensor'), may hold values from -0.21875 to 0.21875
- conv_x: float32 [4, 1536], P(None, 'tensor'), may hold values from -3 to 3
- conv_x_bias: float32 [1536], P('tensor'), may hold values from -3 to 3
- conv_bc: float32 [4, 256], replicated, may hold values from -3 to 3
- conv_bc_bias: float32 [256], replicated, may hold values from -3 to 3
- dt_bias: float32 [24], P('tensor'), may hold values from -5 to -1
- a_log: float32 [24], P('tensor'), may hold values from -4 to 2
- d_skip: float32 [24], P('tensor'), may hold values from 0.5 to 2
- gate_gain: float32 [1536], P('tensor'), may hold values from 0.1 to 1.9
- w_out: bfloat16 [1536, 768], P('tensor'), may hold values from -0.15625 to 0.15625
Outputs:
- result: bfloat16 [8, 512, 768], P('dp')
- grad_x: bfloat16 [8, 512, 768], P('dp')
- grad_norm_gain: float32 [768], replicated
- grad_w_z: float32 [768, 1536], P(None, 'tensor')
- grad_w_x: float32 [768, 1536], P(None, 'tensor')
- grad_w_bc: float32 [768, 256], replicated
- grad_w_dt: float32 [768, 24], P(None, 'tensor')
- grad_conv_x: float32 [4, 1536], P(None, 'tensor')
- grad_conv_x_bias: float32 [1536], P('tensor')
- grad_conv_bc: float32 [4, 256], replicated
- grad_conv_bc_bias: float32 [256], replicated
- grad_dt_bias: float32 [24], P('tensor')
- grad_a_log: float32 [24], P('tensor')
- grad_d_skip: float32 [24], P('tensor')
- grad_gate_gain: float32 [1536], P('tensor')
- grad_w_out: float32 [1536, 768], P('tensor')
All inputs are finite; a program needn't handle non-finite values.
Results may differ from a plain program's by a relative error of at most 0.013.
Values may be sent and summed in bfloat16 or wider, within the bound.
A program may use at most 128 MiB of HBM per device.

v0:
```python
import jax
import jax.numpy as jnp
from jax import lax
from jax.sharding import PartitionSpec as P

Q = 256
epsilon = 1e-05
highest = lax.Precision.HIGHEST


def input_norm(values, norm_gain):
    return (
        values
        * lax.rsqrt(jnp.mean(values * values, axis=-1, keepdims=True) + epsilon)
        * norm_gain[None, :]
    )


def causal_conv(values, kernel, shift_bias):
    length = values.shape[0]
    kernel_taps = kernel.shape[0]
    padded = jnp.pad(values, ((kernel_taps - 1, 0), (0, 0)))
    summed = jnp.zeros_like(values) + shift_bias[None, :]
    for offset in range(kernel_taps):
        summed = summed + kernel[offset][None, :] * padded[offset : offset + length]
    return summed


def state_scan(xheads, b_rows, c_rows, step_size, log_decay):
    length, head_count, head_dim = xheads.shape
    blocks = length // Q
    states = b_rows.shape[1]
    causal_mask = jnp.arange(Q)[:, None] >= jnp.arange(Q)[None, :]

    def advance(carried_state, pieces):
        x_blk, b_blk, c_blk, dt_blk, a_blk = pieces
        cumulative = jnp.cumsum(a_blk, axis=0)
        spread = jnp.where(
            causal_mask[:, :, None], cumulative[:, None, :] - cumulative[None, :, :], -jnp.inf
        )
        scores = jnp.dot(c_blk, b_blk.T, precision=highest)
        mixing = scores[:, :, None] * jnp.exp(spread) * dt_blk[None, :, :]
        inside = jnp.einsum("tsh,shp->thp", mixing, x_blk, precision=highest)
        carried = (
            jnp.einsum("tn,hpn->thp", c_blk, carried_state, precision=highest)
            * jnp.exp(cumulative)[:, :, None]
        )
        weight_tail = jnp.exp(cumulative[-1][None, :] - cumulative) * dt_blk
        update = jnp.einsum(
            "shp,sn->hpn", x_blk * weight_tail[:, :, None], b_blk, precision=highest
        )
        carried_state = carried_state * jnp.exp(cumulative[-1])[:, None, None] + update
        return (carried_state, inside + carried)

    initial = jnp.zeros((head_count, head_dim, states), jnp.float32)
    pieces = (
        xheads.reshape(blocks, Q, head_count, head_dim),
        b_rows.reshape(blocks, Q, states),
        c_rows.reshape(blocks, Q, states),
        step_size.reshape(blocks, Q, head_count),
        log_decay.reshape(blocks, Q, head_count),
    )
    _, outputs = lax.scan(advance, initial, pieces)
    return outputs.reshape(length, head_count, head_dim)


def mixer(
    x_pre, bc_pre, dt_pre, conv_x, conv_x_bias, conv_bc, conv_bc_bias, dt_bias, a_log, d_skip
):
    length, head_count = dt_pre.shape
    xconv = jax.nn.silu(causal_conv(x_pre, conv_x, conv_x_bias))
    bcconv = jax.nn.silu(causal_conv(bc_pre, conv_bc, conv_bc_bias))
    states = bc_pre.shape[1] // 2
    step_size = jax.nn.softplus(dt_pre + dt_bias[None, :])
    log_decay = -step_size * jnp.exp(a_log)[None, :]
    xheads = xconv.reshape(length, head_count, -1)
    mixed = state_scan(xheads, bcconv[:, :states], bcconv[:, states:], step_size, log_decay)
    mixed = mixed + d_skip[None, :, None] * xheads
    return mixed.reshape(length, -1)


def batched_mixer(
    x_pre, bc_pre, dt_pre, conv_x, conv_x_bias, conv_bc, conv_bc_bias, dt_bias, a_log, d_skip
):
    mapped = jax.vmap(mixer, in_axes=(0, 0, 0, None, None, None, None, None, None, None))
    return mapped(
        x_pre, bc_pre, dt_pre, conv_x, conv_x_bias, conv_bc, conv_bc_bias, dt_bias, a_log, d_skip
    )


def silu_slope(values):
    sigmoid = jax.nn.sigmoid(values)
    return sigmoid * (1.0 + values * (1.0 - sigmoid))


def contract_rows(left, right):
    return lax.dot_general(
        left, right, (((0,), (0,)), ((), ())), preferred_element_type=jnp.float32
    )


def contract_cols(left, right):
    return lax.dot_general(
        left, right, (((1,), (1,)), ((), ())), preferred_element_type=jnp.float32
    )


def per_device(
    tokens,
    cotangent,
    norm_gain,
    w_z,
    w_x,
    w_bc,
    w_dt,
    conv_x,
    conv_x_bias,
    conv_bc,
    conv_bc_bias,
    dt_bias,
    a_log,
    d_skip,
    gate_gain,
    w_out,
):
    seq_count, length, width = tokens.shape
    row_count = seq_count * length
    share_rows = row_count // lax.axis_size("tensor")
    first_row = lax.axis_index("tensor") * share_rows
    widef = tokens.reshape(row_count, width).astype(jnp.float32)
    normed = input_norm(widef, norm_gain).astype(jnp.bfloat16)
    gate_pre = jnp.dot(normed, w_z, preferred_element_type=jnp.float32)
    x_pre = jnp.dot(normed, w_x, preferred_element_type=jnp.float32)
    bc_pre = jnp.dot(normed, w_bc, preferred_element_type=jnp.float32)
    dt_pre = jnp.dot(normed, w_dt, preferred_element_type=jnp.float32)
    mixed, mixer_back = jax.vjp(
        batched_mixer,
        x_pre.reshape(seq_count, length, -1),
        bc_pre.reshape(seq_count, length, -1),
        dt_pre.reshape(seq_count, length, -1),
        conv_x,
        conv_x_bias,
        conv_bc,
        conv_bc_bias,
        dt_bias,
        a_log,
        d_skip,
    )
    mixed = mixed.reshape(row_count, -1)
    inner_total = mixed.shape[1] * lax.axis_size("tensor")
    gate_act = jax.nn.silu(gate_pre)
    gated = mixed * gate_act
    squares = lax.psum(jnp.sum(gated * gated, axis=-1), "tensor")
    inverse = lax.rsqrt(squares / inner_total + epsilon)[:, None]
    gated_n = (gated * inverse * gate_gain[None, :]).astype(jnp.bfloat16)
    partial_out = jnp.dot(gated_n, w_out, preferred_element_type=jnp.float32)
    summed_out = lax.psum(partial_out.astype(jnp.bfloat16), "tensor").astype(jnp.float32)
    result = (widef + summed_out).astype(jnp.bfloat16)
    result = result.reshape(seq_count, length, width)
    cotan = cotangent.reshape(row_count, width)
    grad_w_out = contract_rows(gated_n, cotan)
    d_gated_n = contract_cols(cotan, w_out)
    grad_gate_gain = jnp.sum(d_gated_n * gated * inverse, axis=0)
    scaled = gate_gain[None, :] * d_gated_n
    products = lax.psum(jnp.sum(scaled * gated, axis=-1), "tensor")
    d_gated = inverse * scaled - gated * inverse**3 * (products / inner_total)[:, None]
    d_mixed = d_gated * gate_act
    d_gate_pre = d_gated * mixed * silu_slope(gate_pre)
    back = mixer_back(d_mixed.reshape(seq_count, length, -1))
    d_gate_b = d_gate_pre.astype(jnp.bfloat16)
    d_x_b = back[0].reshape(row_count, -1).astype(jnp.bfloat16)
    d_bc_b = back[1].reshape(row_count, -1).astype(jnp.bfloat16)
    d_dt_b = back[2].reshape(row_count, -1).astype(jnp.bfloat16)
    grad_w_z = contract_rows(normed, d_gate_b)
    grad_w_x = contract_rows(normed, d_x_b)
    grad_w_bc = contract_rows(normed, d_bc_b)
    grad_w_dt = contract_rows(normed, d_dt_b)
    d_normed_part = (
        contract_cols(d_gate_b, w_z)
        + contract_cols(d_x_b, w_x)
        + contract_cols(d_bc_b, w_bc)
        + contract_cols(d_dt_b, w_dt)
    )
    input_rows = lax.dynamic_slice_in_dim(widef, first_row, share_rows, 0)
    _, share_back = jax.vjp(input_norm, input_rows, norm_gain)
    d_normed = lax.psum(d_normed_part.astype(jnp.bfloat16), "tensor").astype(jnp.float32)
    _, full_back = jax.vjp(input_norm, widef, norm_gain)
    d_tokens, _ = full_back(d_normed)
    d_normed_rows = lax.dynamic_slice_in_dim(d_normed, first_row, share_rows, 0)
    _, grad_norm_gain = share_back(d_normed_rows)
    grad_x = (cotan.astype(jnp.float32) + d_tokens).astype(jnp.bfloat16)
    grad_x = grad_x.reshape(seq_count, length, width)
    grad_w_bc, grad_conv_bc, grad_conv_bc_bias, grad_norm_gain = lax.psum(
        (grad_w_bc, back[5], back[6], grad_norm_gain), ("dp", "tensor")
    )
    reduced = lax.psum(
        (
            grad_w_z,
            grad_w_x,
            grad_w_dt,
            back[3],
            back[4],
            back[7],
            back[8],
            back[9],
            grad_gate_gain,
            grad_w_out,
        ),
        "dp",
    )
    (
        grad_w_z,
        grad_w_x,
        grad_w_dt,
        grad_conv_x,
        grad_conv_x_bias,
        grad_dt_bias,
        grad_a_log,
        grad_d_skip,
        grad_gate_gain,
        grad_w_out,
    ) = reduced
    return (
        result,
        grad_x,
        grad_norm_gain,
        grad_w_z,
        grad_w_x,
        grad_w_bc,
        grad_w_dt,
        grad_conv_x,
        grad_conv_x_bias,
        grad_conv_bc,
        grad_conv_bc_bias,
        grad_dt_bias,
        grad_a_log,
        grad_d_skip,
        grad_gate_gain,
        grad_w_out,
    )


def solution(mesh):
    placed = (
        P("dp", None, None),
        P("dp", None, None),
        P(),
        P(None, "tensor"),
        P(None, "tensor"),
        P(),
        P(None, "tensor"),
        P(None, "tensor"),
        P("tensor"),
        P(),
        P(),
        P("tensor"),
        P("tensor"),
        P("tensor"),
        P("tensor"),
        P("tensor", None),
    )
    return jax.shard_map(
        per_device,
        mesh=mesh,
        in_specs=placed,
        out_specs=(
            P("dp", None, None),
            P("dp", None, None),
            P(),
            P(None, "tensor"),
            P(None, "tensor"),
            P(),
            P(None, "tensor"),
            P(None, "tensor"),
            P("tensor"),
            P(),
            P(),
            P("tensor"),
            P("tensor"),
            P("tensor"),
            P("tensor"),
            P("tensor", None),
        ),
        check_vma=False,
    )
```

profile of v0, /device:TPU:0, one launch (start us, length us, event | category | flops | bytes accessed | tf_op | source)
XLA Modules:
  0.0 580.4 jit_solution(8823095844115345862)
XLA Ops:
  7.4 1.4 fusion.140
  9.7 1.7 fusion.186
  13.8 1.6 fusion.158
  15.5 1.4 copy.191
  16.9 1.4 reshape.1072
  23.5 54.7 %while.71 = (s32[]{:T(128)}, f32[1,6,64,128]{3,2,1,0:T(8,128)S(1)}, f32[2,1,256,6,64]{2,0,4,3,1:T(2,128)}, f32[2,1,128,256]{2,3,1,0:T(8,128)}, f32[2,1,256,256,6...) while((s32[]{:T(128)}, f32[1,6,64,128]{3,2,1,0:T(8,128)S(1)}, ...), condition=%wide.region_4.5_spmd.clone.clone, body=%wide.region_1.4_spmd.clone.clone.sunk | while | flops 708627456 | bytes 15328889 | solution.py:63
  24.2 1.8 reduce-window.48
  28.7 2.6 multiply_dynamic-update-slice_fusion.4
  34.4 1.9 fusion.284
  36.7 9.0 %dynamic_update_slice.218 = f32[2,1,256,6,64]{2,0,4,3,1:T(2,128)} dynamic-update-slice(f32[2,1,256,6,64]{2,0,4,3,1:T(2,128)} %get-tuple-element.1940, f32[1,1,256,6,64]{2,0,4,3,1:T(1,128)S(1)} %copy.365, s32[]{:T(128)} %get-tuple-element.1938, s32[]{:T(128)} %constant.179.clone.1..sunk.1, s32[]{:T(128)} %constant.179.clone.1..sunk.1, s32[]{:T(128)} %constant.179.clone.1..sunk.1, ...) | dynamic-update-slice | bytes 786436 | tf_op jit(solution)/shard_map/jvp(vmap())/while/body/jit(dynamic_update_index_in_dim)/dynamic_update_slice | solution.py:63
  51.5 1.8 reduce-window.48
  56.0 2.7 multiply_dynamic-update-slice_fusion.4
  61.8 1.9 fusion.284
  64.1 9.0 %dynamic_update_slice.218 = f32[2,1,256,6,64]{2,0,4,3,1:T(2,128)} dynamic-update-slice(f32[2,1,256,6,64]{2,0,4,3,1:T(2,128)} %get-tuple-element.1940, f32[1,1,256,6,64]{2,0,4,3,1:T(1,128)S(1)} %copy.365, s32[]{:T(128)} %get-tuple-element.1938, s32[]{:T(128)} %constant.179.clone.1..sunk.1, s32[]{:T(128)} %constant.179.clone.1..sunk.1, s32[]{:T(128)} %constant.179.clone.1..sunk.1, ...) | dynamic-update-slice | bytes 786436 | tf_op jit(solution)/shard_map/jvp(vmap())/while/body/jit(dynamic_update_index_in_dim)/dynamic_update_slice | solution.py:63
  78.1 2.1 copy.268
  80.2 2.3 copy.197
  82.7 3.4 multiply_reduce_fusion.6
  86.1 9.0 %psum.126 = f32[512]{0:T(512)} all-reduce(f32[512]{0:T(512)S(1)} %get-tuple-element.1483), channel_id=1, replica_groups=mesh['dp'=8,'tensor'=4] {'tensor'}, use_global_device_ids=true, to_apply=%region_6.7 | all-reduce | flops 512 | bytes 4096 | tf_op jit(solution)/shard_map/psum | solution.py:153
  95.9 2.8 convolution_convert_fusion
  98.7 2.1 multiply_reduce_fusion
  100.8 6.0 %psum.128 = f32[512]{0:T(512)S(1)} all-reduce(f32[512]{0:T(512)} %get-tuple-element.1335), channel_id=1, replica_groups=mesh['dp'=8,'tensor'=4] {'tensor'}, use_global_device_ids=true, to_apply=%region_9.10 | all-reduce | flops 512 | bytes 4096 | tf_op jit(solution)/shard_map/psum | solution.py:165
  106.8 4.1 fusion.156
  110.9 1.4 copy.198
  112.4 1.4 reshape_reshape.4
  117.5 114.6 %while.70 = (s32[]{:T(128)}, f32[1,6,64,128]{3,2,1,0:T(8,128)S(1)}, f32[2,1,256,6,64]{2,0,4,3,1:T(2,128)}, f32[2,1,256,128]{3,2,1,0:T(8,128)}, f32[2,1,256,128]{...) while((s32[]{:T(128)}, f32[1,6,64,128]{3,2,1,0:T(8,128)S(1)}, ...), condition=%wide.region_21.22_spmd.clone, body=%wide.region_10.21_spmd.clone.sunk | while | flops 1414609920 | bytes 22201356 | solution.py:63
  117.5 1.6 constant_dynamic-slice_fusion.15
  120.7 4.7 fusion.270
  125.9 1.3 constant_dynamic-slice_fusion.17
  128.6 1.3 copy.357
  130.5 1.3 copy.358
  134.3 1.4 fusion.277
  137.1 8.8 %reduce-window.46 = f32[1,6,2,128]{3,2,1,0:T(2,128)} reduce-window(f32[1,6,2,128]{3,2,1,0:T(2,128)} %bitcast.662, f32[]{:T(128)} %constant.180.clone.1..sunk), window={size=1x1x1x128 pad=0_0x0_0x0_0x0_127}, to_apply=%region_19.19 | reduce-window | flops 195072 | bytes 12292 | tf_op jit(solution)/shard_map/reduce-window.18
  145.9 1.3 copy.359
  149.7 1.4 copy.360
  153.1 1.3 dynamic_update_slice.209
  154.5 1.3 constant_dynamic-slice_fusion.16
  155.8 2.5 fusion.269
  158.7 9.0 %dynamic_update_slice.208 = f32[2,1,256,6,64]{2,0,4,3,1:T(2,128)} dynamic-update-slice(f32[2,1,256,6,64]{2,0,4,3,1:T(2,128)} %get-tuple-element.2025, f32[1,1,256,6,64]{2,0,4,3,1:T(1,128)S(1)} %copy.356, s32[]{:T(128)S(6)} %sub.180, s32[]{:T(128)} %constant.179.clone.1..sunk, s32[]{:T(128)} %constant.179.clone.1..sunk, s32[]{:T(128)} %constant.179.clone.1..sunk, s32[]{:T(128)} %constant.179.clone.1..sunk) | dynamic-update-slice | bytes 786436 | tf_op jit(solution)/shard_map/transpose(jvp(vmap()))/while/body/jit(dynamic_update_index_in_dim)/dynamic_update_slice | solution.py:63
  169.3 2.0 fusion.272
  174.8 1.6 constant_dynamic-slice_fusion.15
  178.0 4.7 fusion.270
  183.2 1.3 constant_dynamic-slice_fusion.17
  191.6 1.4 fusion.277
  194.3 8.8 %reduce-window.46 = f32[1,6,2,128]{3,2,1,0:T(2,128)} reduce-window(f32[1,6,2,128]{3,2,1,0:T(2,128)} %bitcast.662, f32[]{:T(128)} %constant.180.clone.1..sunk), window={size=1x1x1x128 pad=0_0x0_0x0_0x0_127}, to_apply=%region_19.19 | reduce-window | flops 195072 | bytes 12292 | tf_op jit(solution)/shard_map/reduce-window.18
  203.1 1.3 copy.359
  207.0 1.4 copy.360
  210.4 1.3 dynamic_update_slice.209
  211.7 1.3 constant_dynamic-slice_fusion.16
  213.1 2.5 fusion.269
  216.0 9.0 %dynamic_update_slice.208 = f32[2,1,256,6,64]{2,0,4,3,1:T(2,128)} dynamic-update-slice(f32[2,1,256,6,64]{2,0,4,3,1:T(2,128)} %get-tuple-element.2025, f32[1,1,256,6,64]{2,0,4,3,1:T(1,128)S(1)} %copy.356, s32[]{:T(128)S(6)} %sub.180, s32[]{:T(128)} %constant.179.clone.1..sunk, s32[]{:T(128)} %constant.179.clone.1..sunk, s32[]{:T(128)} %constant.179.clone.1..sunk, s32[]{:T(128)} %constant.179.clone.1..sunk) | dynamic-update-slice | bytes 786436 | tf_op jit(solution)/shard_map/transpose(jvp(vmap()))/while/body/jit(dynamic_update_index_in_dim)/dynamic_update_slice | solution.py:63
  226.6 2.0 fusion.272
  232.2 2.2 copy.269
  234.4 2.3 copy.212
  236.7 2.1 multiply_reduce_fusion.3
  247.4 1.4 fusion.178
  248.9 1.7 fusion.180
  250.6 1.7 fusion.182
  252.3 1.6 fusion.151
  257.0 38.6 %all-reduce.23 = (f32[768,6]{0,1:T(8,128)}, f32[4,384]{1,0:T(4,128)}, f32[384]{0:T(512)}, f32[6]{0:T(128)}, f32[6]{0:T(128)}, /*index=5*/f32[6]{0:T(128)}, f32[384]{0:T(512)}) all-reduce(f32[768,6]{0,1:T(8,128)S(1)} %fusion.173, f32[4,384]{1,0:T(4,128)S(1)} %pad_add_fusion.6, ...), channel_id=1, replica_groups=mesh['dp'=8,'tensor'=4] {'dp'}, use_global_device_ids=true, to_apply=%region_30.31 | all-reduce | flops 6930 | bytes 55440 | tf_op jit(solution)/shard_map/psum | solution.py:196
  298.1 37.1 %all-reduce.22 = (f32[768]{0:T(1024)}, f32[4,256]{1,0:T(4,128)}, f32[256]{0:T(256)}) all-reduce(f32[768]{0:T(1024)S(1)} %fusion.166, f32[4,256]{1,0:T(4,128)S(1)} %pad_add_fusion.7, f32[256]{0:T(256)S(1)} %get-tuple-element.1344), channel_id=1, replica_groups=mesh['dp'=8,'tensor'=4] {'dp','tensor'}, use_global_device_ids=true, to_apply=%region_26.27 | all-reduce | flops 2048 | bytes 16384 | tf_op jit(solution)/shard_map/psum | solution.py:193
  335.6 3.2 fusion.149
  338.7 86.3 %all-reduce.30.cloned.1.call-done = f32[768,256]{1,0:T(8,128)} async-done(((f32[768,256]{1,0:T(8,128)}), f32[768,256]{1,0:T(8,128)}) %all-reduce.30.cloned.1.call-update) | async-done | bytes 786448 | tf_op jit(solution)/shard_map/psum | solution.py:193
  425.1 142.8 %all-reduce.32.cloned.1.call-done = (f32[768,384]{1,0:T(8,128)}, f32[768,384]{1,0:T(8,128)}, f32[384,768]{1,0:T(8,128)}) async-done(((f32[768,384]{1,0:T(8,128)}, f32[768,384]{1,0:T(8,128)}, f32[384,768]{1,0:T(8,128)}), (f32[768,384]{1,0:T(8,128)}, f32[768,384]{1,0:T(8,128)}, f32[384,768]{1,0:T(8,128)})) %all-reduce.32.cloned.1.call-update) | async-done | bytes 3538960 | tf_op jit(solution)/shard_map/psum | solution.py:196
  567.9 2.5 copy.471
  (420 shorter events, 92.8 us)
Async XLA Ops:
  7.2 75.5 %copy-start = (bf16[768,384]{1,0:T(8,128)(2,1)S(1)}, bf16[768,384]{1,0:T(8,128)(2,1)}, u32[]{:S(2)}) copy-start(bf16[768,384]{1,0:T(8,128)(2,1)} %param.23) | copy-start | bytes 1769476
  7.2 4.2 copy-start.89
  7.2 288.5 %all-reduce.34.cloned.1.call-start = ((), (), s32[]{:S(2)}) async-start(), calls=%async_computation.2 | async-start | bytes 3145728 | tf_op jit(solution)/shard_map/psum | solution.py:157
  8.8 10.7 %copy-start.83 = (f32[512]{0:T(512)}, f32[512]{0:T(512)S(1)}, u32[]{:S(2)}) copy-start(f32[512]{0:T(512)S(1)} %fusion.176) | copy-start | bytes 6148
  9.7 2.9 copy-start.74
  9.7 2.9 copy-start.76
  9.7 2.9 copy-start.78
  9.7 2.9 copy-start.80
  16.9 2.6 copy-start.72
  19.6 3.9 copy-start.90
  23.5 7.8 %copy-start.28 = (f32[2,1,256,6]{2,3,1,0:T(8,128)}, f32[2,1,256,6]{2,3,1,0:T(8,128)S(1)}, u32[]{:S(2)}) copy-start(f32[2,1,256,6]{2,3,1,0:T(8,128)S(1)} %get-tuple-element.1985) | copy-start | bytes 36868 | tf_op jit(solution)/shard_map/jvp(vmap())/while
  45.7 2.8 copy-start.33
  45.7 2.8 copy-start.39
  45.7 2.9 copy-start.32
  45.7 2.9 copy-start.41
  45.7 2.9 copy-start.43
  45.7 3.0 copy-start.38
  45.7 3.0 copy-start.52
  45.7 4.2 copy-start.34
  45.7 4.2 copy-start.45
  45.7 4.3 copy-start.19
  45.8 5.0 copy-start.29
  50.7 7.9 %copy-start.28 = (f32[2,1,256,6]{2,3,1,0:T(8,128)}, f32[2,1,256,6]{2,3,1,0:T(8,128)S(1)}, u32[]{:S(2)}) copy-start(f32[2,1,256,6]{2,3,1,0:T(8,128)S(1)} %get-tuple-element.1985) | copy-start | bytes 36868 | tf_op jit(solution)/shard_map/jvp(vmap())/while
  73.1 2.8 copy-start.33
  73.1 2.8 copy-start.39
  73.1 2.9 copy-start.32
  73.1 2.9 copy-start.41
  73.1 2.9 copy-start.43
  73.1 3.0 copy-start.38
  73.1 3.0 copy-start.52
  73.1 4.2 copy-start.34
  73.1 4.2 copy-start.45
  73.1 4.3 copy-start.19
  73.1 5.0 copy-start.29
  78.1 4.4 copy-start.30
  78.1 4.4 copy-start.92
  78.1 4.6 copy-start.69
  78.1 4.6 copy-start.84
  82.7 24.1 %copy-start.56 = (f32[384]{0:T(512)}, f32[384]{0:T(512)S(1)}, u32[]{:S(2)}) copy-start(f32[384]{0:T(512)S(1)} %mul.847) | copy-start | bytes 4612
  82.7 13.2 %copy-start.54 = (f32[384]{0:T(512)S(1)}, f32[384]{0:T(512)}, u32[]{:S(2)}) copy-start(f32[384]{0:T(512)} %param.34) | copy-start | bytes 4612
  86.1 12.6 %copy-start.3 = (f32[512,384]{1,0:T(8,128)S(1)}, f32[512,384]{1,0:T(8,128)}, u32[]{:S(2)}) copy-start(f32[512,384]{1,0:T(8,128)} %get-tuple-element.1484) | copy-start | bytes 2359300
  86.1 12.6 %copy-start.15 = (bf16[384,768]{1,0:T(8,128)(2,1)S(1)}, bf16[384,768]{1,0:T(8,128)(2,1)}, u32[]{:S(2)}) copy-start(bf16[384,768]{1,0:T(8,128)(2,1)} %param.35) | copy-start | bytes 1769476
  95.1 3.6 copy-start.11
  95.9 11.0 %copy-start.49 = (f32[512]{0:T(512)}, f32[512]{0:T(512)S(1)}, u32[]{:S(2)}) copy-start(f32[512]{0:T(512)S(1)} %get-tuple-element.1530) | copy-start | bytes 6148
  112.3 5.1 copy-start.7
  117.5 7.9 %copy-start.16 = (pred[256,256]{1,0:T(8,128)(4,1)}, pred[256,256]{1,0:T(8,128)(4,1)S(1)}, u32[]{:S(2)}) copy-start(pred[256,256]{1,0:T(8,128)(4,1)S(1)} %get-tuple-element.2081) | copy-start | bytes 196612 | tf_op jit(solution)/shard_map/transpose(jvp(vmap()))/while
  167.7 5.5 copy-start.14
  167.7 5.5 copy-start.24
  167.7 6.4 %copy-start.96 = (f32[2,1,6,1,1]{2,4,3,1,0:T(1,128)S(1)}, f32[2,1,6,1,1]{2,4,3,1,0:T(1,128)}, u32[]{:S(2)}) copy-start(f32[2,1,6,1,1]{2,4,3,1,0:T(1,128)} %get-tuple-element.2061) | copy-start | bytes 148 | tf_op jit(solution)/shard_map/transpose(jvp(vmap()))/while
  169.3 5.5 copy-start.17
  174.8 7.9 %copy-start.16 = (pred[256,256]{1,0:T(8,128)(4,1)}, pred[256,256]{1,0:T(8,128)(4,1)S(1)}, u32[]{:S(2)}) copy-start(pred[256,256]{1,0:T(8,128)(4,1)S(1)} %get-tuple-element.2081) | copy-start | bytes 196612 | tf_op jit(solution)/shard_map/transpose(jvp(vmap()))/while
  224.9 5.5 copy-start.14
  224.9 5.5 copy-start.24
  224.9 6.4 %copy-start.96 = (f32[2,1,6,1,1]{2,4,3,1,0:T(1,128)S(1)}, f32[2,1,6,1,1]{2,4,3,1,0:T(1,128)}, u32[]{:S(2)}) copy-start(f32[2,1,6,1,1]{2,4,3,1,0:T(1,128)} %get-tuple-element.2061) | copy-start | bytes 148 | tf_op jit(solution)/shard_map/transpose(jvp(vmap()))/while
  226.5 5.5 copy-start.17
  232.2 4.5 copy-start.6
  232.2 4.5 copy-start.13
  232.2 4.5 copy-start.57
  246.3 178.8 %all-reduce.30.cloned.1.call-start = ((), (), s32[]{:S(2)}) async-start(), calls=%async_computation | async-start | bytes 1572864 | tf_op jit(solution)/shard_map/psum | solution.py:193
  248.8 319.1 %all-reduce.32.cloned.1.call-start = ((), (), s32[]{:S(2)}) async-start(), calls=%async_computation.1 | async-start | bytes 7077888 | tf_op jit(solution)/shard_map/psum | solution.py:196
  254.0 2.7 copy-start.95
  254.0 3.0 copy-start.86
  295.7 39.6 %copy-start.10 = (bf16[512,768]{1,0:T(8,128)(2,1)S(1)}, bf16[512,768]{1,0:T(8,128)(2,1)}, u32[]{:S(2)}) copy-start(bf16[512,768]{1,0:T(8,128)(2,1)} %get-tuple-element.1468) | copy-start | bytes 2359300
  297.0 38.6 %copy-start.59 = (f32[512]{0:T(512)S(1)}, f32[512]{0:T(512)}, u32[]{:S(2)}) copy-start(f32[512]{0:T(512)} %copy-done.58) | copy-start | bytes 6148
  (61 other events, 87.6 us)
Sparse Core Ops, SparseCore 0:
  246.4 43.3 all-reduce.33
  295.0 130.0 all-reduce.29
  430.1 137.7 all-reduce.31
where the time goes:
time: 585 us; the launch traced here: 580 us
  waiting for transfers between devices  229 us (39%)
  local copies, waits for them, and re-layouts  118 us (20%)
  blocking collectives  90.8 us (16%)
  other arithmetic  71.2 us (12%)
  matrix products  55.8 us (10%)
  between operations  14.7 us (3%)
    psum x1, waiting for transfers between devices, per_device(): lax.psum((grad_w_z, grad_w_x, grad_w_dt, back[3], back[4], back[7], back[...  143 us
    psum x1, waiting for transfers between devices, per_device(): lax.psum((grad_w_bc, back[5], back[6], grad_norm_gain), ('dp', 'tensor'))  86.3 us
    dynamic_update_slice x26, local copies, waits for them, and re-layouts, state_scan(): _, outputs = lax.scan(advance, initial, pieces)  44.2 us
    psum x1, blocking collectives, per_device(): lax.psum((grad_w_z, grad_w_x, grad_w_dt, back[3], back[4], back[7], back[...  38.6 us
    psum x1, blocking collectives, per_device(): lax.psum((grad_w_bc, back[5], back[6], grad_norm_gain), ('dp', 'tensor'))  37.1 us
    another operation x19, other arithmetic  26.7 us
    another operation x28, local copies, waits for them, and re-layouts  18.7 us
    dot_general x6, matrix products, advance(): inside = jnp.einsum('tsh,shp->thp', mixing, x_blk, precision=highest)  18.1 us
  transfers between devices with their start and end apart: 3, of which 2 were waited for; matrix products, arithmetic and copies ran while one was open for 3% of the time, Pallas kernels for 0%

commit v1 on v0

--- a/solution.py
+++ b/solution.py
@@ -191,7 +191,7 @@
     grad_x = (cotan.astype(jnp.float32) + d_tokens).astype(jnp.bfloat16)
     grad_x = grad_x.reshape(seq_count, length, width)
     grad_w_bc, grad_conv_bc, grad_conv_bc_bias, grad_norm_gain = lax.psum(
-        (grad_w_bc, back[5], back[6], grad_norm_gain), ("dp", "tensor")
+        lax.psum((grad_w_bc, back[5], back[6], grad_norm_gain), axis_name="tensor"), axis_name="dp"
     )
     reduced = lax.psum(
         (

time: 585 us -> 462 us (0.79)
  waiting for transfers between devices: 229 us -> 170 us
  blocking collectives: 90.8 us -> 61.8 us
  local copies, waits for them, and re-layouts: 118 us -> 94.1 us
  other arithmetic: 71.2 us -> 55.8 us
    psum x1, waiting for transfers between devices: 86.3 us -> 14.4 us  [per_device(): lax.psum((grad_w_bc, back[5], back[6], grad_norm_gain), axis_name='tensor')]
    psum x1, waiting for transfers between devices: 0.02 us -> 42.8 us  [per_device(): lax.psum(partial_out.astype(jnp.bfloat16), 'tensor').astype(jnp.float32)]
    psum x1, waiting for transfers between devices: 143 us -> 113 us  [per_device(): lax.psum((grad_w_z, grad_w_x, grad_w_dt, back[3], back[4], back[7], back[...]
    psum x2, blocking collectives: 75.7 us -> 47.4 us  [the longest x1 41.3 us: per_device(): lax.psum(lax.psum((grad_w_bc, back[5], back[6], grad_norm_gain), axis_nam...]
    another operation x28, local copies, waits for them, and re-layouts: 18.7 us -> 7.29 us
    another operation x19, other arithmetic: 26.7 us -> 19.1 us
    unnamed x152 -> x138, local copies, waits for them, and re-layouts: 16 us -> 15.6 us
  transfers between devices with their start and end apart: 3 -> 3, of which waited for: 2 -> 3; matrix products, arithmetic and copies ran while one was open for 3% -> 6% of each run, Pallas kernels for 0% -> 0%
where the time goes in v1:
time: 462 us; the launch traced here: 458 us
  waiting for transfers between devices  170 us (37%)
  local copies, waits for them, and re-layouts  94.1 us (20%)
  blocking collectives  61.8 us (13%)
  matrix products  60 us (13%)
  other arithmetic  55.8 us (12%)
  between operations  14.6 us (3%)
    psum x1, waiting for transfers between devices, per_device(): lax.psum((grad_w_z, grad_w_x, grad_w_dt, back[3], back[4], back[7], back[...  113 us
    dynamic_update_slice x26, local copies, waits for them, and re-layouts, state_scan(): _, outputs = lax.scan(advance, initial, pieces)  43 us
    psum x1, waiting for transfers between devices, per_device(): lax.psum(partial_out.astype(jnp.bfloat16), 'tensor').astype(jnp.float32)  42.8 us
    psum x1, blocking collectives, per_device(): lax.psum(lax.psum((grad_w_bc, back[5], back[6], grad_norm_gain), axis_nam...  41.3 us
    another operation x19, other arithmetic  19.1 us
    dot_general x6, matrix products, advance(): inside = jnp.einsum('tsh,shp->thp', mixing, x_blk, precision=highest)  16.8 us
    unnamed x138, local copies, waits for them, and re-layouts  15.6 us
    psum x1, waiting for transfers between devices, per_device(): lax.psum((grad_w_bc, back[5], back[6], grad_norm_gain), axis_name='tensor')  14.4 us
  transfers between devices with their start and end apart: 3, of which 3 were waited for; matrix products, arithmetic and copies ran while one was open for 6% of the time, Pallas kernels for 0%

profile of v1, /device:TPU:0, one launch (start us, length us, event | category | flops | bytes accessed | tf_op | source)
XLA Modules:
  0.0 457.5 jit_solution(2325202235306323347)
XLA Ops:
  7.4 1.4 fusion.140
  9.7 1.7 fusion.186
  13.8 1.6 fusion.158
  15.4 1.4 copy.191
  16.9 1.4 reshape.1072
  18.2 1.2 copy.192
  23.4 56.0 %while.71 = (s32[]{:T(128)}, f32[1,6,64,128]{3,2,1,0:T(8,128)S(1)}, f32[2,1,256,6,64]{2,0,4,3,1:T(2,128)}, f32[2,1,128,256]{2,3,1,0:T(8,128)}, f32[2,1,256,256,6...) while((s32[]{:T(128)}, f32[1,6,64,128]{3,2,1,0:T(8,128)S(1)}, ...), condition=%wide.region_4.5_spmd.clone.clone, body=%wide.region_1.4_spmd.clone.clone.sunk | while | flops 708627456 | bytes 15232577 | solution.py:63
  24.1 1.8 reduce-window.48
  28.1 1.3 bitcast_dynamic-update-slice_fusion.10
  29.4 2.6 multiply_dynamic-update-slice_fusion.4
  33.8 1.2 bitcast_dynamic-update-slice_fusion.12
  35.0 1.9 fusion.284
  37.4 9.0 %dynamic_update_slice.218 = f32[2,1,256,6,64]{2,0,4,3,1:T(2,128)} dynamic-update-slice(f32[2,1,256,6,64]{2,0,4,3,1:T(2,128)} %get-tuple-element.1944, f32[1,1,256,6,64]{2,0,4,3,1:T(1,128)S(1)} %copy.365, s32[]{:T(128)} %get-tuple-element.1942, s32[]{:T(128)} %constant.179.clone.1..sunk.1, s32[]{:T(128)} %constant.179.clone.1..sunk.1, s32[]{:T(128)} %constant.179.clone.1..sunk.1, ...) | dynamic-update-slice | bytes 786436 | tf_op jit(solution)/shard_map/jvp(vmap())/while/body/jit(dynamic_update_index_in_dim)/dynamic_update_slice | solution.py:63
  52.1 1.8 reduce-window.48
  56.0 1.3 bitcast_dynamic-update-slice_fusion.10
  57.3 2.7 multiply_dynamic-update-slice_fusion.4
  61.9 1.2 bitcast_dynamic-update-slice_fusion.12
  63.1 1.9 fusion.284
  65.5 9.0 %dynamic_update_slice.218 = f32[2,1,256,6,64]{2,0,4,3,1:T(2,128)} dynamic-update-slice(f32[2,1,256,6,64]{2,0,4,3,1:T(2,128)} %get-tuple-element.1944, f32[1,1,256,6,64]{2,0,4,3,1:T(1,128)S(1)} %copy.365, s32[]{:T(128)} %get-tuple-element.1942, s32[]{:T(128)} %constant.179.clone.1..sunk.1, s32[]{:T(128)} %constant.179.clone.1..sunk.1, s32[]{:T(128)} %constant.179.clone.1..sunk.1, ...) | dynamic-update-slice | bytes 786436 | tf_op jit(solution)/shard_map/jvp(vmap())/while/body/jit(dynamic_update_index_in_dim)/dynamic_update_slice | solution.py:63
  79.5 2.1 copy.268
  81.6 2.3 copy.197
  84.0 3.4 multiply_reduce_fusion.6
  87.4 8.5 %psum.154 = f32[512]{0:T(512)S(1)} all-reduce(f32[512]{0:T(512)S(1)} %get-tuple-element.1487), channel_id=1, replica_groups=mesh['dp'=8,'tensor'=4] {'tensor'}, use_global_device_ids=true, to_apply=%region_6.7 | all-reduce | flops 512 | bytes 4096 | tf_op jit(solution)/shard_map/psum | solution.py:153
  95.9 3.6 multiply_reduce_fusion
  99.5 5.9 %psum.156 = f32[512]{0:T(512)S(1)} all-reduce(f32[512]{0:T(512)S(1)} %get-tuple-element.1335), channel_id=1, replica_groups=mesh['dp'=8,'tensor'=4] {'tensor'}, use_global_device_ids=true, to_apply=%region_9.10 | all-reduce | flops 512 | bytes 4096 | tf_op jit(solution)/shard_map/psum | solution.py:165
  105.5 4.2 fusion.156
  109.6 1.4 copy.198
  111.0 1.4 reshape_reshape.4
  116.1 76.4 %while.70 = (s32[]{:T(128)}, f32[1,6,64,128]{3,2,1,0:T(8,128)S(1)}, f32[2,1,256,6,64]{2,0,4,3,1:T(2,128)}, f32[2,1,256,128]{3,2,1,0:T(8,128)}, f32[2,1,256,128]{...) while((s32[]{:T(128)}, f32[1,6,64,128]{3,2,1,0:T(8,128)S(1)}, ...), condition=%wide.region_21.22_spmd.clone, body=%wide.region_10.21_spmd.clone.sunk | while | flops 1414609920 | bytes 19924064 | solution.py:63
  116.1 1.5 constant_dynamic-slice_fusion.15
  119.4 4.0 fusion.270
  127.9 7.6 %reduce-window.46 = f32[1,6,2,128]{3,2,1,0:T(2,128)S(1)} reduce-window(f32[1,6,2,128]{3,2,1,0:T(2,128)S(1)} %bitcast.662, f32[]{:T(128)} %constant.180.clone.1..sunk), window={size=1x1x1x128 pad=0_0x0_0x0_0x0_127}, to_apply=%region_19.19 | reduce-window | flops 195072 | bytes 12292 | tf_op jit(solution)/shard_map/reduce-window.18
  135.9 2.5 fusion.269
  138.8 9.0 %dynamic_update_slice.208 = f32[2,1,256,6,64]{2,0,4,3,1:T(2,128)} dynamic-update-slice(f32[2,1,256,6,64]{2,0,4,3,1:T(2,128)} %get-tuple-element.2029, f32[1,1,256,6,64]{2,0,4,3,1:T(1,128)S(1)} %copy.356, s32[]{:T(128)S(6)} %sub.180, s32[]{:T(128)} %constant.179.clone.1..sunk, s32[]{:T(128)} %constant.179.clone.1..sunk, s32[]{:T(128)} %constant.179.clone.1..sunk, s32[]{:T(128)} %constant.179.clone.1..sunk) | dynamic-update-slice | bytes 786436 | tf_op jit(solution)/shard_map/transpose(jvp(vmap()))/while/body/jit(dynamic_update_index_in_dim)/dynamic_update_slice | solution.py:63
  147.8 1.8 convolution_bitcast_fusion.9
  149.6 1.9 fusion.272
  152.2 1.5 fusion.271
  154.2 1.5 constant_dynamic-slice_fusion.15
  157.5 4.0 fusion.270
  166.0 7.6 %reduce-window.46 = f32[1,6,2,128]{3,2,1,0:T(2,128)S(1)} reduce-window(f32[1,6,2,128]{3,2,1,0:T(2,128)S(1)} %bitcast.662, f32[]{:T(128)} %constant.180.clone.1..sunk), window={size=1x1x1x128 pad=0_0x0_0x0_0x0_127}, to_apply=%region_19.19 | reduce-window | flops 195072 | bytes 12292 | tf_op jit(solution)/shard_map/reduce-window.18
  174.0 2.5 fusion.269
  176.9 9.0 %dynamic_update_slice.208 = f32[2,1,256,6,64]{2,0,4,3,1:T(2,128)} dynamic-update-slice(f32[2,1,256,6,64]{2,0,4,3,1:T(2,128)} %get-tuple-element.2029, f32[1,1,256,6,64]{2,0,4,3,1:T(1,128)S(1)} %copy.356, s32[]{:T(128)S(6)} %sub.180, s32[]{:T(128)} %constant.179.clone.1..sunk, s32[]{:T(128)} %constant.179.clone.1..sunk, s32[]{:T(128)} %constant.179.clone.1..sunk, s32[]{:T(128)} %constant.179.clone.1..sunk) | dynamic-update-slice | bytes 786436 | tf_op jit(solution)/shard_map/transpose(jvp(vmap()))/while/body/jit(dynamic_update_index_in_dim)/dynamic_update_slice | solution.py:63
  185.9 1.8 convolution_bitcast_fusion.9
  187.7 1.9 fusion.272
  190.2 1.5 fusion.271
  192.6 2.6 multiply_reduce_fusion.9
  196.5 1.4 fusion.178
  198.0 2.6 fusion.202
  200.6 1.5 convolution_convert_fusion
  203.1 2.3 copy.212
  205.4 2.3 multiply_reduce_fusion.3
  211.9 1.3 add_convert_fusion
  214.2 1.7 fusion.180
  215.9 1.7 fusion.182
  217.6 1.6 fusion.151
  219.2 14.4 %all-reduce.30.cloned.1.call-done = f32[768,256]{1,0:T(8,128)} async-done(((f32[768,256]{1,0:T(8,128)}), f32[768,256]{1,0:T(8,128)}) %all-reduce.30.cloned.1.call-update) | async-done | bytes 786448 | tf_op jit(solution)/shard_map/psum | solution.py:194
  233.6 1.3 convert_element_type.69
  236.7 42.8 %all-reduce.34.cloned.1.call-done = (bf16[512,768]{1,0:T(8,128)(2,1)}, bf16[512,768]{1,0:T(8,128)(2,1)}) async-done(((bf16[512,768]{1,0:T(8,128)(2,1)}, bf16[512,768]{1,0:T(8,128)(2,1)}), (bf16[512,768]{1,0:T(8,128)(2,1)}, bf16[512,768]{1,0:T(8,128)(2,1)})) %all-reduce.34.cloned.1.call-update) | async-done | bytes 1572880 | tf_op jit(solution)/shard_map/psum | solution.py:157
  279.4 1.3 convert_element_type.84
  281.9 6.0 %all-reduce.24 = (f32[768]{0:T(1024)S(1)}, f32[4,256]{1,0:T(4,128)S(1)}, f32[256]{0:T(256)S(1)}) all-reduce(f32[768]{0:T(1024)S(1)} %fusion.166, f32[4,256]{1,0:T(4,128)S(1)} %pad_add_fusion.7, f32[256]{0:T(256)S(1)} %get-tuple-element.1344), channel_id=1, replica_groups=mesh['dp'=8,'tensor'=4] {'tensor'}, use_global_device_ids=true, to_apply=%region_26.27 | all-reduce | flops 2048 | bytes 16384 | tf_op jit(solution)/shard_map/psum | solution.py:194
  287.9 41.3 %all-reduce.22 = (f32[768]{0:T(1024)}, f32[768,6]{0,1:T(8,128)}, f32[4,384]{1,0:T(4,128)}, f32[384]{0:T(512)}, f32[4,256]{1,0:T(4,128)}, /*index=5*/f32[256]{0:T...) all-reduce(f32[768]{0:T(1024)S(1)} %get-tuple-element.1468, ...), channel_id=1, replica_groups=mesh['dp'=8,'tensor'=4] {'dp'}, use_global_device_ids=true, to_apply=%region_27.28 | all-reduce | flops 8978 | bytes 71824 | tf_op jit(solution)/shard_map/psum | solution.py:193
  330.4 1.8 fusion.149
  332.2 112.9 %all-reduce.32.cloned.1.call-done = (f32[768,384]{1,0:T(8,128)}, f32[768,384]{1,0:T(8,128)}, f32[768,256]{1,0:T(8,128)}, f32[384,768]{1,0:T(8,128)}) async-done(((f32[768,384]{1,0:T(8,128)}, f32[768,384]{1,0:T(8,128)}, f32[768,256]{1,0:T(8,128)}, f32[384,768]{1,0:T(8,128)}), (f32[768,384]{1,0:T(8,128)}, f32[768,384]{1,0:T(8,128)}, f32[768,256]{1,0:T(8,128)}, ...) | async-done | bytes 4325392 | tf_op jit(solution)/shard_map/psum | solution.py:196
  445.1 2.5 copy.472
  (410 shorter events, 61.9 us)
Async XLA Ops:
  7.2 76.8 %copy-start = (bf16[768,384]{1,0:T(8,128)(2,1)S(1)}, bf16[768,384]{1,0:T(8,128)(2,1)}, u32[]{:S(2)}) copy-start(bf16[768,384]{1,0:T(8,128)(2,1)} %param.23) | copy-start | bytes 1769476
  7.2 4.2 copy-start.83
  7.2 226.4 %all-reduce.30.cloned.1.call-start = ((), (), s32[]{:S(2)}) async-start(), calls=%async_computation | async-start | bytes 1572864 | tf_op jit(solution)/shard_map/psum | solution.py:194
  8.8 10.7 %copy-start.77 = (f32[512]{0:T(512)}, f32[512]{0:T(512)S(1)}, u32[]{:S(2)}) copy-start(f32[512]{0:T(512)S(1)} %fusion.176) | copy-start | bytes 6148
  9.7 2.9 copy-start.68
  9.7 2.9 copy-start.70
  9.7 2.9 copy-start.72
  9.7 2.9 copy-start.74
  16.9 2.6 copy-start.66
  19.5 3.9 copy-start.84
  46.3 2.8 copy-start.25
  46.3 2.8 copy-start.30
  46.3 2.9 copy-start.24
  46.3 2.9 copy-start.32
  46.4 2.9 copy-start.34
  46.4 3.0 copy-start.29
  46.4 3.0 copy-start.47
  46.4 4.2 copy-start.26
  46.4 4.2 copy-start.37
  46.4 4.3 copy-start.14
  74.4 2.8 copy-start.25
  74.4 2.8 copy-start.30
  74.4 2.9 copy-start.24
  74.4 2.9 copy-start.32
  74.4 2.9 copy-start.34
  74.4 3.0 copy-start.29
  74.5 3.0 copy-start.47
  74.5 4.2 copy-start.26
  74.5 4.2 copy-start.37
  74.5 4.2 copy-start.14
  79.5 4.4 copy-start.86
  79.5 4.5 copy-start.63
  79.5 4.5 copy-start.78
  84.0 21.4 %copy-start.50 = (f32[384]{0:T(512)}, f32[384]{0:T(512)S(1)}, u32[]{:S(2)}) copy-start(f32[384]{0:T(512)S(1)} %mul.847) | copy-start | bytes 4612
  84.0 11.9 %copy-start.49 = (f32[384]{0:T(512)S(1)}, f32[384]{0:T(512)}, u32[]{:S(2)}) copy-start(f32[384]{0:T(512)} %param.34) | copy-start | bytes 4612
  87.4 18.1 %copy-start.3 = (f32[512,384]{1,0:T(8,128)S(1)}, f32[512,384]{1,0:T(8,128)}, u32[]{:S(2)}) copy-start(f32[512,384]{1,0:T(8,128)} %get-tuple-element.1488) | copy-start | bytes 2359300
  119.4 5.2 %copy-start.21 = (f32[2,1,256,6]{2,3,1,0:T(8,128)S(1)}, f32[2,1,256,6]{2,3,1,0:T(8,128)}, u32[]{:S(2)}) copy-start(f32[2,1,256,6]{2,3,1,0:T(8,128)} %get-tuple-element.2081) | copy-start | bytes 36868 | tf_op jit(solution)/shard_map/transpose(jvp(vmap()))/while
  123.3 12.4 %copy-start.44 = (f32[2,1,256,6]{2,0,3,1:T(2,128)S(1)}, f32[2,1,256,6]{2,0,3,1:T(2,128)}, u32[]{:S(2)}) copy-start(f32[2,1,256,6]{2,0,3,1:T(2,128)} %get-tuple-element.2033) | copy-start | bytes 36868 | tf_op jit(solution)/shard_map/transpose(jvp(vmap()))/while
  123.3 12.5 %copy-start.36 = (f32[2,1,256,6,1]{2,0,4,3,1:T(2,128)S(1)}, f32[2,1,256,6,1]{2,0,4,3,1:T(2,128)}, u32[]{:S(2)}) copy-start(f32[2,1,256,6,1]{2,0,4,3,1:T(2,128)} %get-tuple-element.2070) | copy-start | bytes 36868 | tf_op jit(solution)/shard_map/transpose(jvp(vmap()))/while
  123.3 12.5 %copy-start.39 = (f32[2,1,256,6,1]{2,0,4,3,1:T(2,128)S(1)}, f32[2,1,256,6,1]{2,0,4,3,1:T(2,128)}, u32[]{:S(2)}) copy-start(f32[2,1,256,6,1]{2,0,4,3,1:T(2,128)} %get-tuple-element.2067) | copy-start | bytes 36868 | tf_op jit(solution)/shard_map/transpose(jvp(vmap()))/while
  135.8 3.0 copy-start.45
  138.4 13.2 %copy-start.40 = (f32[2,1,256,6]{2,3,1,0:T(8,128)S(1)}, f32[2,1,256,6]{2,3,1,0:T(8,128)}, u32[]{:S(2)}) copy-start(f32[2,1,256,6]{2,3,1,0:T(8,128)} %get-tuple-element.2032) | copy-start | bytes 36868 | tf_op jit(solution)/shard_map/transpose(jvp(vmap()))/while
  147.8 4.4 copy-start.11
  147.8 5.9 %copy-start.90 = (f32[2,1,6,1,1]{2,4,3,1,0:T(1,128)S(1)}, f32[2,1,6,1,1]{2,4,3,1,0:T(1,128)}, u32[]{:S(2)}) copy-start(f32[2,1,6,1,1]{2,4,3,1,0:T(1,128)} %get-tuple-element.2065) | copy-start | bytes 148 | tf_op jit(solution)/shard_map/transpose(jvp(vmap()))/while
  151.5 2.7 copy-start.41
  157.5 5.2 %copy-start.21 = (f32[2,1,256,6]{2,3,1,0:T(8,128)S(1)}, f32[2,1,256,6]{2,3,1,0:T(8,128)}, u32[]{:S(2)}) copy-start(f32[2,1,256,6]{2,3,1,0:T(8,128)} %get-tuple-element.2081) | copy-start | bytes 36868 | tf_op jit(solution)/shard_map/transpose(jvp(vmap()))/while
  161.4 12.4 %copy-start.44 = (f32[2,1,256,6]{2,0,3,1:T(2,128)S(1)}, f32[2,1,256,6]{2,0,3,1:T(2,128)}, u32[]{:S(2)}) copy-start(f32[2,1,256,6]{2,0,3,1:T(2,128)} %get-tuple-element.2033) | copy-start | bytes 36868 | tf_op jit(solution)/shard_map/transpose(jvp(vmap()))/while
  161.4 12.5 %copy-start.36 = (f32[2,1,256,6,1]{2,0,4,3,1:T(2,128)S(1)}, f32[2,1,256,6,1]{2,0,4,3,1:T(2,128)}, u32[]{:S(2)}) copy-start(f32[2,1,256,6,1]{2,0,4,3,1:T(2,128)} %get-tuple-element.2070) | copy-start | bytes 36868 | tf_op jit(solution)/shard_map/transpose(jvp(vmap()))/while
  161.4 12.5 %copy-start.39 = (f32[2,1,256,6,1]{2,0,4,3,1:T(2,128)S(1)}, f32[2,1,256,6,1]{2,0,4,3,1:T(2,128)}, u32[]{:S(2)}) copy-start(f32[2,1,256,6,1]{2,0,4,3,1:T(2,128)} %get-tuple-element.2067) | copy-start | bytes 36868 | tf_op jit(solution)/shard_map/transpose(jvp(vmap()))/while
  173.9 3.0 copy-start.45
  176.5 13.2 %copy-start.40 = (f32[2,1,256,6]{2,3,1,0:T(8,128)S(1)}, f32[2,1,256,6]{2,3,1,0:T(8,128)}, u32[]{:S(2)}) copy-start(f32[2,1,256,6]{2,3,1,0:T(8,128)} %get-tuple-element.2032) | copy-start | bytes 36868 | tf_op jit(solution)/shard_map/transpose(jvp(vmap()))/while
  185.9 4.4 copy-start.11
  185.9 5.9 %copy-start.90 = (f32[2,1,6,1,1]{2,4,3,1,0:T(1,128)S(1)}, f32[2,1,6,1,1]{2,4,3,1,0:T(1,128)}, u32[]{:S(2)}) copy-start(f32[2,1,6,1,1]{2,4,3,1,0:T(1,128)} %get-tuple-element.2065) | copy-start | bytes 148 | tf_op jit(solution)/shard_map/transpose(jvp(vmap()))/while
  189.6 2.7 copy-start.41
  197.9 2.7 copy-start.4
  197.9 2.7 copy-start.13
  197.9 81.5 %all-reduce.34.cloned.1.call-start = ((), (), s32[]{:S(2)}) async-start(), calls=%async_computation.2 | async-start | bytes 3145728 | tf_op jit(solution)/shard_map/psum | solution.py:157
  202.1 3.3 copy-start.6
  202.1 3.3 copy-start.51
  213.2 231.9 %all-reduce.32.cloned.1.call-start = ((), (), s32[]{:S(2)}) async-start(), calls=%async_computation.1 | async-start | bytes 8650752 | tf_op jit(solution)/shard_map/psum | solution.py:196
  233.6 2.7 copy-start.89
  279.4 8.5 %copy-start.80 = (f32[384]{0:T(512)S(1)}, f32[384]{0:T(512)}, u32[]{:S(2)}) copy-start(f32[384]{0:T(512)} %get-tuple-element.1334) | copy-start | bytes 4612
  279.4 49.8 %copy-start.8 = (bf16[512,768]{1,0:T(8,128)(2,1)S(1)}, bf16[512,768]{1,0:T(8,128)(2,1)}, u32[]{:S(2)}) copy-start(bf16[512,768]{1,0:T(8,128)(2,1)} %get-tuple-element.1472) | copy-start | bytes 2359300
  280.8 48.9 %copy-start.53 = (f32[512]{0:T(512)S(1)}, f32[512]{0:T(512)}, u32[]{:S(2)}) copy-start(f32[512]{0:T(512)} %copy-done.52) | copy-start | bytes 6148
  (56 other events, 85.8 us)
Sparse Core Ops, SparseCore 0:
  198.1 35.4 all-reduce.29
  236.5 42.8 all-reduce.33
  284.5 160.5 all-reduce.31
